TPU v7x, 32 devices: a whole 2x2x4 slice. The times are simulated.
32 devices in a mesh: grp: 2 (over y), wide: 4 (over z), narrow: 2 (over x), tile: 2 (over core).
Axes of the slice: x: 2, y: 2, z: 4, core: 2. Of those that a mesh axis runs over, the one named last changes fastest.
Arguments:
- green: bfloat16 [32768, 1024], P(('grp', 'wide', 'narrow', 'tile')), parts along dimension 0, may hold values from -0.52734375 to 0.52734375
- log_strength: float32 [32768], P(('grp', 'wide', 'narrow', 'tile')), parts along dimension 0, may hold values from -1 to 1
- observed: float32 [1056, 512], P('grp'), parts along dimension 0, may hold values from -6 to 6
- owner_map: int32 [1056], P('grp'), parts along dimension 0, may hold values from 0 to 527, each once
Outputs:
- new_log_strength: float32 [32768], P(('grp', 'wide', 'narrow', 'tile')), parts along dimension 0
- residual: float32 [1056, 512], P(('grp', 'wide')), parts along dimension 0
There are 2 independent parts, one for each index of `grp`. A program takes and returns all parts, laid end to end along the dimension named above; each array names one. Nothing has to cross between parts.
Inputs may be any that keep to these rules, and one draw needn't show every extreme that they name: `owner_map`: every tile number appears once; the slots form 4 equal runs in order, the k-th run owned by the k-th index of wide.
All inputs are finite; a program needn't handle non-finite values.
Results may differ from a plain program's by a relative error of at most 0.0018.
Values may be sent and summed in bfloat16 or wider, within the bound.
A program may use at most 64 MiB of HBM per device.

v0:
```python
import functools

import jax
import jax.numpy as jnp
import numpy as np
from jax import lax
from jax.experimental import pallas as pl
from jax.experimental.pallas import tpu as pltpu
from jax.sharding import PartitionSpec as P

NB = 32
STEPS = 2
LANES = 128
MESH = pl.DeviceIdType.MESH
F32, BF16 = jnp.float32, jnp.bfloat16


def upper_blocks(count):
    return [(g, c) for g in range(count) for c in range(g, count)]


def slot_table(blocks, width):
    per_lane = LANES // width
    index = {gc: b for b, gc in enumerate(upper_blocks(blocks * width // LANES))}
    rows, cols = np.triu_indices(blocks)
    units = [index[(i // per_lane, j // per_lane)] * per_lane + i % per_lane for i, j in zip(rows, cols)]
    return np.asarray(units, np.int32), np.asarray(cols % per_lane, np.int32)


def pieces(axis_sizes, units):
    n_wide, n_narrow, n_tile = axis_sizes
    total = n_wide * n_narrow * n_tile
    return -(-units // total)


def kernel(
    sizes, send_types,
    green_ref, log_ref, observed_ref, owner_ref, unit_ref, lane_ref,
    new_log_ref, out_ref,
    green_t, weighted_t, spectra, half, half_send, quarter, quarter_send, own_observed,
    re_kernel, im_kernel, gathered, gathered_low, staged_re, staged_im,
    recv_tile, recv_narrow, recv_wide,
    rs_send, rs_recv, ag_send, ag_recv,
):
    n_wide, n_narrow, n_tile = sizes
    ns = green_ref.shape[1] // 2
    width = ns // NB
    per_lane = LANES // width
    blocks = upper_blocks(ns // LANES)
    re_units = len(blocks) * per_lane
    flat = width * width
    per = pieces(sizes, 2 * re_units)
    w, n, t = lax.axis_index("wide"), lax.axis_index("narrow"), lax.axis_index("tile")
    axes = (("tile", n_tile, t), ("narrow", n_narrow, n), ("wide", n_wide, w))

    barrier = pltpu.get_barrier_semaphore()
    for name, size, me in axes:
        for o in range(1, size):
            pl.semaphore_signal(barrier, inc=1, device_id={name: lax.rem(me + o, size)}, device_id_type=MESH)
    pl.semaphore_wait(barrier, n_tile + n_narrow + n_wide - 3)

    green_t[...] = green_ref[...].T

    narrow_units = n_wide * per
    tile_units = n_narrow * narrow_units
    my_quarter = t * tile_units + n * narrow_units
    my_first = my_quarter + w * per

    def unit_facts(u):
        part = jnp.where(u >= re_units, 1, 0) + jnp.where(u >= 2 * re_units, 1, 0)
        v = jnp.where(part == 2, 0, u - part * re_units)
        b = v // per_lane
        g, c = jnp.int32(0), b
        first = 0
        for row in range(1, ns // LANES):
            first += ns // LANES - row + 1
            g = jnp.where(b >= first, row, g)
            c = jnp.where(b >= first, b - first + row, c)
        return part, g * per_lane + v % per_lane, c

    lane = lax.broadcasted_iota(jnp.int32, (width, per_lane, LANES), 2)
    place = lax.broadcasted_iota(jnp.int32, (width, per_lane, LANES), 1)
    in_place = lane // width == place
    entry = lax.broadcasted_iota(jnp.int32, (width, per_lane, flat), 2)
    row_of = lax.broadcasted_iota(jnp.int32, (width, per_lane, flat), 0)
    in_row = entry // width == row_of
    fold_a = lax.broadcasted_iota(jnp.int32, (flat, LANES), 0)
    fold_b = lax.broadcasted_iota(jnp.int32, (flat, LANES), 1)
    fold = jnp.where(fold_a % width == fold_b % width, 1.0, 0.0).astype(BF16)

    for e in range(per):
        part, i, c = unit_facts(my_first + e)
        start = i * NB - (i * (i - 1)) // 2 + c * per_lane - i
        both = jnp.concatenate([observed_ref[pl.ds(start + j, 1), :] for j in range(per_lane)], axis=0)
        tiles = jnp.where(part == 1, both[:, flat:], both[:, :flat])
        spread = jnp.where(in_row, tiles[None], 0.0).reshape(width * per_lane, flat)
        high = spread.astype(BF16)
        low = (spread - high.astype(F32)).astype(BF16)
        lanes = jnp.dot(high, fold, preferred_element_type=F32) + jnp.dot(low, fold, preferred_element_type=F32)
        own_observed[e] = jnp.sum(jnp.where(in_place, lanes.reshape(width, per_lane, LANES), 0.0), axis=1)

    for ref in (re_kernel, im_kernel):
        ref[...] = jnp.zeros_like(ref)
    pad_units = spectra.shape[0] - 2 * re_units
    if pad_units:
        spectra[2 * re_units:] = jnp.zeros((pad_units, width, LANES), F32)

    wide_rows = 2 * LANES
    row_groups = [(r, slice(r, r + wide_rows)) for r in range(0, ns, wide_rows)]

    def copies(src_of, dst_of, name, size, me, send, recv, base):
        out = []
        for o in range(1, size):
            to = lax.rem(me + o, size)
            out.append(pltpu.make_async_remote_copy(
                src_ref=src_of(to), dst_ref=dst_of(o), send_sem=send.at[base + o - 1], recv_sem=recv.at[base + o - 1],
                device_id={name: to}, device_id_type=MESH))
        for copy in out:
            copy.start()
        return out

    def wait(started):
        for copy in started:
            copy.wait()

    per_pass = n_tile + n_narrow + n_wide - 3
    at_narrow, at_wide = n_tile - 1, n_tile + n_narrow - 2
    log_now = log_ref[...]
    for step in range(STEPS):
        last = step == STEPS - 1
        strength = jnp.exp(log_now)
        weighted_t[...] = (green_t[...].astype(F32) * strength).astype(BF16)
        for r, rows in row_groups:
            rows_b = slice(ns + r, ns + r + wide_rows)
            wa, wb = weighted_t[rows, :], weighted_t[rows_b, :]
            ga, gb = green_ref[:, r:ns], green_ref[:, ns + r:]
            real = jnp.dot(wa, ga, preferred_element_type=F32) + jnp.dot(wb, gb, preferred_element_type=F32)
            imag = jnp.dot(wb, ga, preferred_element_type=F32) - jnp.dot(wa, gb, preferred_element_type=F32)
            for b, (g, c) in enumerate(blocks):
                if r <= g * LANES < r + wide_rows:
                    at = (slice(g * LANES - r, (g + 1) * LANES - r), slice(c * LANES - r, (c + 1) * LANES - r))
                    spectra[b * per_lane:(b + 1) * per_lane] = real[at].reshape(per_lane, width, LANES)
                    first = re_units + b * per_lane
                    spectra[first:first + per_lane] = imag[at].reshape(per_lane, width, LANES)

        base = step * per_pass
        wait(copies(
            lambda to: spectra.at[pl.ds(to * tile_units, tile_units)], lambda o: recv_tile.at[step, o - 1],
            "tile", n_tile, t, rs_send, rs_recv, base))
        total = spectra[pl.ds(t * tile_units, tile_units)]
        for o in range(n_tile - 1):
            total = total + recv_tile[step, o]
        half[...] = total
        source = half_send[step] if half_send[step] is not None else half
        if source is not half:
            source[...] = total.astype(source.dtype)
        wait(copies(
            lambda to: source.at[pl.ds(to * narrow_units, narrow_units)], lambda o: recv_narrow[step].at[o - 1],
            "narrow", n_narrow, n, rs_send, rs_recv, base + at_narrow))
        total = half[pl.ds(n * narrow_units, narrow_units)]
        for o in range(n_narrow - 1):
            total = total + recv_narrow[step][o].astype(F32)
        quarter[...] = total
        source = quarter_send[step] if quarter_send[step] is not None else quarter
        if source is not quarter:
            source[...] = total.astype(source.dtype)
        wait(copies(
            lambda to: source.at[pl.ds(to * per, per)], lambda o: recv_wide[step].at[o - 1],
            "wide", n_wide, w, rs_send, rs_recv, base + at_wide))
        total = quarter[pl.ds(w * per, per)]
        for o in range(n_wide - 1):
            total = total + recv_wide[step][o].astype(F32)
        residual = jnp.tanh(total - own_observed[...])

        column = lax.broadcasted_iota(jnp.int32, (width, LANES), 1) // width
        kept = []
        for e in range(per):
            part, i, c = unit_facts(my_first + e)
            limit = jnp.where(part == 2, NB, i)
            kept.append(jnp.where(column + c * per_lane >= limit, residual[e], 0.0))
        residual = jnp.stack(kept)
        high = residual.astype(BF16)
        mine = pl.ds(my_first, per)
        gathered[step, mine] = high
        if last:
            gathered_low[mine] = (residual - high.astype(F32)).astype(BF16)

        def gather(ref, name, size, me, first, units, at):
            view = ref.at[pl.ds(first, units)]
            return copies(lambda to: view, lambda o: view, name, size, me, ag_send, ag_recv, at)

        hi = gathered.at[step]
        base_low = STEPS * per_pass
        run = gather(hi, "wide", n_wide, w, my_first, per, base + at_wide)
        if last:
            low_run = gather(gathered_low, "wide", n_wide, w, my_first, per, base_low + at_wide)
        wait(run)
        wait(gather(hi, "narrow", n_narrow, n, my_quarter, narrow_units, base + at_narrow))
        run = gather(hi, "tile", n_tile, t, t * tile_units, tile_units, base)
        if last:
            wait(low_run)
            low_run = gather(gathered_low, "narrow", n_narrow, n, my_quarter, narrow_units, base_low + at_narrow)
        wait(run)

        for b, (g, c) in enumerate(blocks):
            at = (slice(g * LANES, (g + 1) * LANES), slice(c * LANES, (c + 1) * LANES))
            re_kernel[at] = gathered[step, b * per_lane:(b + 1) * per_lane].reshape(LANES, LANES)
            first = re_units + b * per_lane
            im_kernel[at] = gathered[step, first:first + per_lane].reshape(LANES, LANES)
        contraction = jnp.zeros_like(log_now)
        for r, rows in row_groups:
            rows_b = slice(ns + r, ns + r + wide_rows)
            a, b = green_t[r:ns, :], green_t[ns + r:, :]
            re, im = re_kernel[rows, r:ns], im_kernel[rows, r:ns]
            top = jnp.dot(re, a, preferred_element_type=F32) - jnp.dot(im, b, preferred_element_type=F32)
            bottom = jnp.dot(im, a, preferred_element_type=F32) + jnp.dot(re, b, preferred_element_type=F32)
            terms = green_t[rows, :].astype(F32) * top + green_t[rows_b, :].astype(F32) * bottom
            contraction = contraction + jnp.sum(terms, axis=0, keepdims=True)
        log_now = log_now - 0.5 * strength * contraction

    new_log_ref[...] = log_now
    wait(low_run)
    wait(gather(gathered_low, "tile", n_tile, t, t * tile_units, tile_units, base_low))

    slots = out_ref.shape[0]
    lane_group = lax.broadcasted_iota(jnp.int32, (width, LANES), 1) // width

    def stage(k, carry):
        tile = owner_ref[w * slots + k]
        unit, group = unit_ref[tile], lane_ref[tile]
        keep = lane_group == group
        for ref, offset in ((staged_re, 0), (staged_im, re_units)):
            for part, source in enumerate((gathered.at[STEPS - 1], gathered_low)):
                value = jnp.where(keep, source[unit + offset].astype(F32), 0.0)
                ref[k, :, part * LANES:(part + 1) * LANES] = value.astype(BF16)
        return carry

    lax.fori_loop(0, slots, stage, 0)
    unfold_a = lax.broadcasted_iota(jnp.int32, (2 * LANES, flat), 0)
    unfold_b = lax.broadcasted_iota(jnp.int32, (2 * LANES, flat), 1)
    unfold = jnp.where(unfold_a % width == unfold_b % width, 1.0, 0.0).astype(BF16)
    row = lax.broadcasted_iota(jnp.int32, (1, width, flat), 1)
    col = lax.broadcasted_iota(jnp.int32, (1, width, flat), 2)
    diagonal = col // width == row
    for part, ref in enumerate((staged_re, staged_im)):
        rows = ref[...].reshape(slots * width, 2 * LANES)
        spread = jnp.dot(rows, unfold, preferred_element_type=F32).reshape(slots, width, flat)
        out_ref[:, part * flat:(part + 1) * flat] = jnp.sum(jnp.where(diagonal, spread, 0.0), axis=1)


def solution(mesh):
    sizes = (mesh.shape["wide"], mesh.shape["narrow"], mesh.shape["tile"])
    n_wide, n_narrow, n_tile = sizes
    send_types = (F32,) * STEPS

    def on_device(green, log_strength, observed, owner_map):
        points, stations = green.shape
        ns = stations // 2
        width = ns // NB
        flat = width * width
        per_lane = LANES // width
        slots = owner_map.shape[0] // n_wide
        units = 2 * len(upper_blocks(ns // LANES)) * per_lane
        per = pieces(sizes, units)
        narrow_units = n_wide * per
        tile_units = n_narrow * narrow_units
        all_units = n_tile * tile_units
        per_pass = n_tile + n_narrow + n_wide - 3

        def buf(lead, kind):
            return pltpu.VMEM((*lead, width, LANES), kind)

        vmem, smem = pl.BlockSpec(memory_space=pltpu.VMEM), pl.BlockSpec(memory_space=pltpu.SMEM)
        unit_table, lane_table = slot_table(NB, width)
        sems = pltpu.SemaphoreType.DMA
        new_log, residual = pl.pallas_call(
            functools.partial(kernel, sizes, send_types),
            out_shape=(
                jax.ShapeDtypeStruct((1, points), F32),
                jax.ShapeDtypeStruct((slots, 2 * flat), F32),
            ),
            in_specs=[vmem] * 3 + [smem] * 3,
            out_specs=(vmem, vmem),
            scratch_shapes=[
                pltpu.VMEM((stations, points), BF16),
                pltpu.VMEM((stations, points), BF16),
                buf((all_units,), F32),
                buf((tile_units,), F32),
                tuple(None if k == F32 else buf((tile_units,), k) for k in send_types),
                buf((narrow_units,), F32),
                tuple(None if k == F32 else buf((narrow_units,), k) for k in send_types),
                buf((per,), F32),
                pltpu.VMEM((ns, ns), BF16),
                pltpu.VMEM((ns, ns), BF16),
                buf((STEPS, all_units), BF16),
                buf((all_units,), BF16),
                pltpu.VMEM((slots, width, 2 * LANES), BF16),
                pltpu.VMEM((slots, width, 2 * LANES), BF16),
                buf((STEPS, n_tile - 1, tile_units), F32),
                tuple(buf((n_narrow - 1, narrow_units), k) for k in send_types),
                tuple(buf((n_wide - 1, per), k) for k in send_types),
                sems((STEPS * per_pass,)),
                sems((STEPS * per_pass,)),
                sems(((STEPS + 1) * per_pass,)),
                sems(((STEPS + 1) * per_pass,)),
            ],
            compiler_params=pltpu.CompilerParams(
                collective_id=0, has_side_effects=True, vmem_limit_bytes=60 * 1024 * 1024
            ),
        )(green, log_strength[None, :], observed, owner_map, jnp.asarray(unit_table), jnp.asarray(lane_table))
        return new_log[0], residual

    parts = ("grp", "wide", "narrow", "tile")
    return jax.shard_map(
        on_device, mesh=mesh, in_specs=(P(parts, None), P(parts), P("grp", None), P("grp")),
        out_specs=(P(parts), P(("grp", "wide"), None)), check_vma=False,
    )
```

profile of v0, /device:TPU:0, one launch (start us, length us, event | category | flops | bytes accessed | tf_op | source)
XLA Modules:
  0.0 87.0 jit_solution(4172907878055524131)
XLA Ops:
  0.6 83.4 %shard_map.77 = (f32[1,1024]{1,0:T(1,128)}, f32[132,512]{1,0:T(8,128)}) custom-call(bf16[1024,1024]{1,0:T(8,128)(2,1)} %green_ref.1, f32[1,1024]{1,0:T(1,128)} %bitcast.2, f32[528,512]{1,0:T(8,128)} %observed_ref.1, s32[528]{0:T(1024)} %owner_ref.1, s32[528]{0:T(1024)} %constant.4.clone.unit_ref, s32[528]{0:T(1024)} %constant.5.clone.lane_ref), custom_call_target="tpu_custom_call" | custom-call | tf_op jit(solution)/shard_map/pallas_call | solution.py:276
  84.1 1.3 %copy.10 = f32[1024]{0:T(1024)} copy(f32[1024]{0:T(1024)} %bitcast.3) | data formatting | bytes 8192
  85.4 1.7 %copy.11 = f32[132,512]{1,0:T(8,128)} copy(f32[132,512]{1,0:T(8,128)} %get-tuple-element.9) | data formatting | bytes 540672
where the time goes:
time: 87.2 us; the launch traced here: 87 us
  Pallas kernels  83.4 us (96%)
  local copies, waits for them, and re-layouts  2.96 us (3%)
    pallas_call x1, Pallas kernels, on_device(): pl.pallas_call(functools.partial(kernel, sizes, send_types), out_shape=(j...  83.4 us
    unnamed x2, local copies, waits for them, and re-layouts  2.96 us

commit v1 on v0

v1 whole, which is shorter than its diff:
```python
import functools

import jax
import jax.numpy as jnp
import numpy as np
from jax import lax
from jax.experimental import pallas as pl
from jax.experimental.pallas import tpu as pltpu
from jax.sharding import PartitionSpec as P

NB = 32
STEPS = 2
LANES = 128
MESH = pl.DeviceIdType.MESH
F32, BF16 = jnp.float32, jnp.bfloat16


def upper_blocks(count):
    return [(g, c) for g in range(count) for c in range(g, count)]


def slot_table(blocks, width):
    per_lane = LANES // width
    index = {gc: b for b, gc in enumerate(upper_blocks(blocks * width // LANES))}
    rows, cols = np.triu_indices(blocks)
    units = [index[(i // per_lane, j // per_lane)] * per_lane + i % per_lane for i, j in zip(rows, cols)]
    return np.asarray(units, np.int32), np.asarray(cols % per_lane, np.int32)


def piece_units(sizes, units):
    n_wide, n_narrow, n_tile = sizes
    return -(-units // (n_wide * n_narrow * n_tile))


def kernel(
    sizes,
    green_ref, log_ref, observed_ref, owner_ref, unit_ref, lane_ref,
    new_log_ref, out_ref,
    green_t, weighted_t, spectra, half, half_send, quarter, quarter_send, own_observed,
    kernels, gathered, gathered_low, staged_re, staged_im,
    recv_tile, recv_narrow, recv_wide,
    rs_send, rs_recv, ag_send, ag_recv,
):
    n_wide, n_narrow, n_tile = sizes
    ns = green_ref.shape[1] // 2
    width = ns // NB
    per_lane = LANES // width
    blocks = upper_blocks(ns // LANES)
    units = len(blocks) * per_lane
    flat = width * width
    per = piece_units(sizes, units)
    w, n, t = lax.axis_index("wide"), lax.axis_index("narrow"), lax.axis_index("tile")
    places = {"tile": (n_tile, t), "narrow": (n_narrow, n), "wide": (n_wide, w)}

    barrier = pltpu.get_barrier_semaphore()
    for name, (size, me) in places.items():
        for o in range(1, size):
            pl.semaphore_signal(barrier, inc=1, device_id={name: lax.rem(me + o, size)}, device_id_type=MESH)
    pl.semaphore_wait(barrier, n_tile + n_narrow + n_wide - 3)

    green_t[...] = green_ref[...].T

    narrow_units = n_wide * per
    tile_units = n_narrow * narrow_units
    my_tile = t * tile_units
    my_quarter = my_tile + n * narrow_units
    my_first = my_quarter + w * per

    def unit_facts(u):
        padding = u >= units
        v = jnp.where(padding, 0, u)
        b = v // per_lane
        g, c = jnp.int32(0), b
        first = 0
        for row in range(1, ns // LANES):
            first += ns // LANES - row + 1
            g = jnp.where(b >= first, row, g)
            c = jnp.where(b >= first, b - first + row, c)
        return padding, g * per_lane + v % per_lane, c

    def lay_out_observed():
        lane = lax.broadcasted_iota(jnp.int32, (width, per_lane, LANES), 2)
        place = lax.broadcasted_iota(jnp.int32, (width, per_lane, LANES), 1)
        in_place = lane // width == place
        entry = lax.broadcasted_iota(jnp.int32, (width, per_lane, flat), 2)
        row_of = lax.broadcasted_iota(jnp.int32, (width, per_lane, flat), 0)
        in_row = entry // width == row_of
        fold_a = lax.broadcasted_iota(jnp.int32, (flat, LANES), 0)
        fold_b = lax.broadcasted_iota(jnp.int32, (flat, LANES), 1)
        fold = jnp.where(fold_a % width == fold_b % width, 1.0, 0.0).astype(BF16)
        for e in range(per):
            _, i, c = unit_facts(my_first + e)
            start = i * NB - (i * (i - 1)) // 2 + c * per_lane - i
            both = jnp.concatenate([observed_ref[pl.ds(start + j, 1), :] for j in range(per_lane)], axis=0)
            for part in range(2):
                tiles = both[:, part * flat:(part + 1) * flat]
                spread = jnp.where(in_row, tiles[None], 0.0).reshape(width * per_lane, flat)
                high = spread.astype(BF16)
                low = (spread - high.astype(F32)).astype(BF16)
                lanes = jnp.dot(high, fold, preferred_element_type=F32) + jnp.dot(low, fold, preferred_element_type=F32)
                lanes = lanes.reshape(width, per_lane, LANES)
                own_observed[part, e] = jnp.sum(jnp.where(in_place, lanes, 0.0), axis=1)

    wide_rows = 2 * LANES
    row_groups = [(r, slice(r, r + wide_rows)) for r in range(0, ns, wide_rows)]
    per_pass = n_tile + n_narrow + n_wide - 3
    offsets = {"tile": 0, "narrow": n_tile - 1, "wide": n_tile + n_narrow - 2}
    pending = []

    def copies(src_of, dst_of, name, send, recv, group):
        size, me = places[name]
        base = group * per_pass + offsets[name] - 1
        out = []
        for o in range(1, size):
            to = lax.rem(me + o, size)
            out.append(pltpu.make_async_remote_copy(
                src_ref=src_of(to), dst_ref=dst_of(o), send_sem=send.at[base + o], recv_sem=recv.at[base + o],
                device_id={name: to}, device_id_type=MESH))
        for copy in out:
            copy.start()
        pending.extend(out)
        return out

    def arrive(started):
        for copy in started:
            copy.wait_recv()

    def gather(ref, name, group):
        first, count = {
            "wide": (my_first, per), "narrow": (my_quarter, narrow_units), "tile": (my_tile, tile_units),
        }[name]
        view = ref.at[pl.ds(first, count)]
        return copies(lambda to: view, lambda o: view, name, ag_send, ag_recv, group)

    log_now = log_ref[...]
    for step in range(STEPS):
        last = step == STEPS - 1
        strength = jnp.exp(log_now)
        weighted_t[...] = (green_t[...].astype(F32) * strength).astype(BF16)
        run = [None, None]
        for part in range(2):
            for r, rows in row_groups:
                wa, wb = weighted_t[rows, :], weighted_t[slice(ns + r, ns + r + wide_rows), :]
                ga, gb = green_ref[:, r:ns], green_ref[:, ns + r:]
                if part == 0:
                    value = jnp.dot(wa, ga, preferred_element_type=F32) + jnp.dot(wb, gb, preferred_element_type=F32)
                else:
                    value = jnp.dot(wb, ga, preferred_element_type=F32) - jnp.dot(wa, gb, preferred_element_type=F32)
                for b, (g, c) in enumerate(blocks):
                    if r <= g * LANES < r + wide_rows:
                        at = (slice(g * LANES - r, (g + 1) * LANES - r), slice(c * LANES - r, (c + 1) * LANES - r))
                        spectra[part, b * per_lane:(b + 1) * per_lane] = value[at].reshape(per_lane, width, LANES)
            pad_units = spectra.shape[1] - units
            if pad_units and step == 0:
                spectra[part, units:] = jnp.zeros((pad_units, width, LANES), F32)
            run[part] = copies(
                lambda to: spectra.at[part, pl.ds(to * tile_units, tile_units)], lambda o: recv_tile.at[step, part, o - 1],
                "tile", rs_send, rs_recv, 2 * step + part)
        if step == 0:
            lay_out_observed()
            kernels[...] = jnp.zeros_like(kernels)
        for part in range(2):
            arrive(run[part])
            total = spectra[part, pl.ds(my_tile, tile_units)]
            for o in range(n_tile - 1):
                total = total + recv_tile[step, part, o]
            half[part] = total
            source = half
            if half_send[step] is not None:
                source = half_send[step]
                source[part] = total.astype(source.dtype)
            run[part] = copies(
                lambda to: source.at[part, pl.ds(to * narrow_units, narrow_units)],
                lambda o: recv_narrow[step].at[part, o - 1], "narrow", rs_send, rs_recv, 2 * step + part)
        for part in range(2):
            arrive(run[part])
            total = half[part, pl.ds(n * narrow_units, narrow_units)]
            for o in range(n_narrow - 1):
                total = total + recv_narrow[step][part, o].astype(F32)
            quarter[part] = total
            source = quarter
            if quarter_send[step] is not None:
                source = quarter_send[step]
                source[part] = total.astype(source.dtype)
            run[part] = copies(
                lambda to: source.at[part, pl.ds(to * per, per)],
                lambda o: recv_wide[step].at[part, o - 1], "wide", rs_send, rs_recv, 2 * step + part)
        column = lax.broadcasted_iota(jnp.int32, (width, LANES), 1) // width
        for part in range(2):
            arrive(run[part])
            total = quarter[part, pl.ds(w * per, per)]
            for o in range(n_wide - 1):
                total = total + recv_wide[step][part, o].astype(F32)
            residual = jnp.tanh(total - own_observed[part])
            kept = []
            for e in range(per):
                padding, i, c = unit_facts(my_first + e)
                limit = jnp.where(padding, NB, i)
                kept.append(jnp.where(column + c * per_lane >= limit, residual[e], 0.0))
            residual = jnp.stack(kept)
            high = residual.astype(BF16)
            gathered[step, part, pl.ds(my_first, per)] = high
            if last:
                gathered_low[part, pl.ds(my_first, per)] = (residual - high.astype(F32)).astype(BF16)
            run[part] = gather(gathered.at[step, part], "wide", 2 * step + part)
        low_run = [None, None]

        def low_stage(name):
            if last:
                for part in range(2):
                    if low_run[part] is not None:
                        arrive(low_run[part])
                    low_run[part] = gather(gathered_low.at[part], name, 2 * STEPS + part)

        low_stage("wide")
        for name in ("narrow", "tile"):
            for part in range(2):
                arrive(run[part])
                run[part] = gather(gathered.at[step, part], name, 2 * step + part)
        contraction = jnp.zeros_like(log_now)
        for part in range(2):
            arrive(run[part])
            low_stage(("narrow", "tile")[part])
            for b, (g, c) in enumerate(blocks):
                at = (slice(g * LANES, (g + 1) * LANES), slice(c * LANES, (c + 1) * LANES))
                kernels[(part, *at)] = gathered[step, part, b * per_lane:(b + 1) * per_lane].reshape(LANES, LANES)
            for r, rows in row_groups:
                block = kernels[part, rows, r:ns]
                from_a = jnp.dot(block, green_t[r:ns, :], preferred_element_type=F32)
                from_b = jnp.dot(block, green_t[ns + r:, :], preferred_element_type=F32)
                a = green_t[rows, :].astype(F32)
                b = green_t[slice(ns + r, ns + r + wide_rows), :].astype(F32)
                terms = a * from_a + b * from_b if part == 0 else b * from_a - a * from_b
                contraction = contraction + jnp.sum(terms, axis=0, keepdims=True)
        log_now = log_now - 0.5 * strength * contraction
        for copy in pending:
            copy.wait_send()
        pending.clear()

    new_log_ref[...] = log_now
    for part in range(2):
        arrive(low_run[part])

    slots = out_ref.shape[0]
    lane_group = lax.broadcasted_iota(jnp.int32, (width, LANES), 1) // width

    def stage(k, carry):
        tile = owner_ref[w * slots + k]
        unit, group = unit_ref[tile], lane_ref[tile]
        keep = lane_group == group
        for part, ref in enumerate((staged_re, staged_im)):
            for side, source in enumerate((gathered.at[STEPS - 1, part], gathered_low.at[part])):
                value = jnp.where(keep, source[unit].astype(F32), 0.0)
                ref[k, :, side * LANES:(side + 1) * LANES] = value.astype(BF16)
        return carry

    lax.fori_loop(0, slots, stage, 0)
    unfold_a = lax.broadcasted_iota(jnp.int32, (2 * LANES, flat), 0)
    unfold_b = lax.broadcasted_iota(jnp.int32, (2 * LANES, flat), 1)
    unfold = jnp.where(unfold_a % width == unfold_b % width, 1.0, 0.0).astype(BF16)
    row = lax.broadcasted_iota(jnp.int32, (1, width, flat), 1)
    col = lax.broadcasted_iota(jnp.int32, (1, width, flat), 2)
    diagonal = col // width == row
    for part, ref in enumerate((staged_re, staged_im)):
        rows = ref[...].reshape(slots * width, 2 * LANES)
        spread = jnp.dot(rows, unfold, preferred_element_type=F32).reshape(slots, width, flat)
        out_ref[:, part * flat:(part + 1) * flat] = jnp.sum(jnp.where(diagonal, spread, 0.0), axis=1)


def solution(mesh):
    sizes = (mesh.shape["wide"], mesh.shape["narrow"], mesh.shape["tile"])
    n_wide, n_narrow, n_tile = sizes
    send_types = (F32,) * STEPS

    def on_device(green, log_strength, observed, owner_map):
        points, stations = green.shape
        ns = stations // 2
        width = ns // NB
        flat = width * width
        per_lane = LANES // width
        slots = owner_map.shape[0] // n_wide
        units = len(upper_blocks(ns // LANES)) * per_lane
        per = piece_units(sizes, units)
        narrow_units = n_wide * per
        tile_units = n_narrow * narrow_units
        all_units = n_tile * tile_units
        per_pass = n_tile + n_narrow + n_wide - 3

        def buf(lead, kind):
            return pltpu.VMEM((*lead, width, LANES), kind)

        vmem, smem = pl.BlockSpec(memory_space=pltpu.VMEM), pl.BlockSpec(memory_space=pltpu.SMEM)
        unit_table, lane_table = slot_table(NB, width)
        sems = pltpu.SemaphoreType.DMA
        new_log, residual = pl.pallas_call(
            functools.partial(kernel, sizes),
            out_shape=(
                jax.ShapeDtypeStruct((1, points), F32),
                jax.ShapeDtypeStruct((slots, 2 * flat), F32),
            ),
            in_specs=[vmem] * 3 + [smem] * 3,
            out_specs=(vmem, vmem),
            scratch_shapes=[
                pltpu.VMEM((stations, points), BF16),
                pltpu.VMEM((stations, points), BF16),
                buf((2, all_units), F32),
                buf((2, tile_units), F32),
                tuple(None if k == F32 else buf((2, tile_units), k) for k in send_types),
                buf((2, narrow_units), F32),
                tuple(None if k == F32 else buf((2, narrow_units), k) for k in send_types),
                buf((2, per), F32),
                pltpu.VMEM((2, ns, ns), BF16),
                buf((STEPS, 2, all_units), BF16),
                buf((2, all_units), BF16),
                pltpu.VMEM((slots, width, 2 * LANES), BF16),
                pltpu.VMEM((slots, width, 2 * LANES), BF16),
                buf((STEPS, 2, n_tile - 1, tile_units), F32),
                tuple(buf((2, n_narrow - 1, narrow_units), k) for k in send_types),
                tuple(buf((2, n_wide - 1, per), k) for k in send_types),
                sems((2 * STEPS * per_pass,)),
                sems((2 * STEPS * per_pass,)),
                sems((2 * (STEPS + 1) * per_pass,)),
                sems((2 * (STEPS + 1) * per_pass,)),
            ],
            compiler_params=pltpu.CompilerParams(
                collective_id=0, has_side_effects=True, vmem_limit_bytes=60 * 1024 * 1024
            ),
        )(green, log_strength[None, :], observed, owner_map, jnp.asarray(unit_table), jnp.asarray(lane_table))
        return new_log[0], residual

    parts = ("grp", "wide", "narrow", "tile")
    return jax.shard_map(
        on_device, mesh=mesh, in_specs=(P(parts, None), P(parts), P("grp", None), P("grp")),
        out_specs=(P(parts), P(("grp", "wide"), None)), check_vma=False,
    )
```

time: 87.2 us -> 76.9 us (0.88)
  Pallas kernels: 83.4 us -> 73.2 us
    pallas_call x1, Pallas kernels: 83.4 us -> 73.2 us  [on_device(): pl.pallas_call(functools.partial(kernel, sizes), out_shape=(jax.ShapeDtyp...]
where the time goes in v1:
time: 76.9 us; the launch traced here: 76.8 us
  Pallas kernels  73.2 us (95%)
  local copies, waits for them, and re-layouts  2.96 us (4%)
    pallas_call x1, Pallas kernels, on_device(): pl.pallas_call(functools.partial(kernel, sizes), out_shape=(jax.ShapeDtyp...  73.2 us
    unnamed x2, local copies, waits for them, and re-layouts  2.96 us

profile of v1, /device:TPU:0, one launch (start us, length us, event | category | flops | bytes accessed | tf_op | source)
XLA Modules:
  0.0 76.8 jit_solution(7609767191553102371)
XLA Ops:
  0.6 73.2 %shard_map.77 = (f32[1,1024]{1,0:T(1,128)}, f32[132,512]{1,0:T(8,128)}) custom-call(bf16[1024,1024]{1,0:T(8,128)(2,1)} %green_ref.1, f32[1,1024]{1,0:T(1,128)} %bitcast.2, f32[528,512]{1,0:T(8,128)} %observed_ref.1, s32[528]{0:T(1024)} %owner_ref.1, s32[528]{0:T(1024)} %constant.4.clone.unit_ref, s32[528]{0:T(1024)} %constant.5.clone.lane_ref), custom_call_target="tpu_custom_call" | custom-call | tf_op jit(solution)/shard_map/pallas_call | solution.py:295
  73.8 1.3 %copy.10 = f32[1024]{0:T(1024)} copy(f32[1024]{0:T(1024)} %bitcast.3) | data formatting | bytes 8192
  75.1 1.7 %copy.11 = f32[132,512]{1,0:T(8,128)} copy(f32[132,512]{1,0:T(8,128)} %get-tuple-element.9) | data formatting | bytes 540672

commit v2 on v1

--- a/solution.py
+++ b/solution.py
@@ -270,7 +270,7 @@
 def solution(mesh):
     sizes = (mesh.shape["wide"], mesh.shape["narrow"], mesh.shape["tile"])
     n_wide, n_narrow, n_tile = sizes
-    send_types = (F32,) * STEPS
+    send_types = (BF16,) * (STEPS - 1) + (F32,)
 
     def on_device(green, log_strength, observed, owner_map):
         points, stations = green.shape

time: 76.9 us -> 70.9 us (0.922)
  Pallas kernels: 73.2 us -> 67.1 us
    pallas_call x1, Pallas kernels: 73.2 us -> 67.1 us  [on_device(): pl.pallas_call(functools.partial(kernel, sizes), out_shape=(jax.ShapeDtyp...]
where the time goes in v2:
time: 70.9 us; the launch traced here: 70.7 us
  Pallas kernels  67.1 us (95%)
  local copies, waits for them, and re-layouts  2.96 us (4%)
    pallas_call x1, Pallas kernels, on_device(): pl.pallas_call(functools.partial(kernel, sizes), out_shape=(jax.ShapeDtyp...  67.1 us
    unnamed x2, local copies, waits for them, and re-layouts  2.96 us

profile of v2, /device:TPU:0, one launch (start us, length us, event | category | flops | bytes accessed | tf_op | source)
XLA Modules:
  0.0 70.7 jit_solution(10731658305831824566)
XLA Ops:
  0.6 67.1 %shard_map.77 = (f32[1,1024]{1,0:T(1,128)}, f32[132,512]{1,0:T(8,128)}) custom-call(bf16[1024,1024]{1,0:T(8,128)(2,1)} %green_ref.1, f32[1,1024]{1,0:T(1,128)} %bitcast.2, f32[528,512]{1,0:T(8,128)} %observed_ref.1, s32[528]{0:T(1024)} %owner_ref.1, s32[528]{0:T(1024)} %constant.4.clone.unit_ref, s32[528]{0:T(1024)} %constant.5.clone.lane_ref), custom_call_target="tpu_custom_call" | custom-call | tf_op jit(solution)/shard_map/pallas_call | solution.py:295
  67.7 1.3 %copy.10 = f32[1024]{0:T(1024)} copy(f32[1024]{0:T(1024)} %bitcast.3) | data formatting | bytes 8192
  69.0 1.7 %copy.11 = f32[132,512]{1,0:T(8,128)} copy(f32[132,512]{1,0:T(8,128)} %get-tuple-element.9) | data formatting | bytes 540672

commit v3 on v2

--- a/solution.py
+++ b/solution.py
@@ -36,7 +36,7 @@
     sizes,
     green_ref, log_ref, observed_ref, owner_ref, unit_ref, lane_ref,
     new_log_ref, out_ref,
-    green_t, weighted_t, spectra, half, half_send, quarter, quarter_send, own_observed,
+    green_t, weighted_t, spectra, spectra_send, half, half_send, quarter, quarter_send, own_observed,
     kernels, gathered, gathered_low, staged_re, staged_im,
     recv_tile, recv_narrow, recv_wide,
     rs_send, rs_recv, ag_send, ag_recv,
@@ -138,7 +138,9 @@
         strength = jnp.exp(log_now)
         weighted_t[...] = (green_t[...].astype(F32) * strength).astype(BF16)
         run = [None, None]
-        for part in range(2):
+        first_source = spectra if spectra_send[step] is None else spectra_send[step]
+        for part in range(2):
+            source = first_source
             for r, rows in row_groups:
                 wa, wb = weighted_t[rows, :], weighted_t[slice(ns + r, ns + r + wide_rows), :]
                 ga, gb = green_ref[:, r:ns], green_ref[:, ns + r:]
@@ -149,12 +151,16 @@
                 for b, (g, c) in enumerate(blocks):
                     if r <= g * LANES < r + wide_rows:
                         at = (slice(g * LANES - r, (g + 1) * LANES - r), slice(c * LANES - r, (c + 1) * LANES - r))
-                        spectra[part, b * per_lane:(b + 1) * per_lane] = value[at].reshape(per_lane, width, LANES)
+                        block = value[at].reshape(per_lane, width, LANES)
+                        spectra[part, b * per_lane:(b + 1) * per_lane] = block
+                        if source is not spectra:
+                            source[part, b * per_lane:(b + 1) * per_lane] = block.astype(source.dtype)
             pad_units = spectra.shape[1] - units
-            if pad_units and step == 0:
-                spectra[part, units:] = jnp.zeros((pad_units, width, LANES), F32)
+            for ref in {id(r): r for r in (spectra, source)}.values():
+                if pad_units and (step == 0 or ref is not spectra):
+                    ref[part, units:] = jnp.zeros((pad_units, width, LANES), ref.dtype)
             run[part] = copies(
-                lambda to: spectra.at[part, pl.ds(to * tile_units, tile_units)], lambda o: recv_tile.at[step, part, o - 1],
+                lambda to: source.at[part, pl.ds(to * tile_units, tile_units)], lambda o: recv_tile[step].at[part, o - 1],
                 "tile", rs_send, rs_recv, 2 * step + part)
         if step == 0:
             lay_out_observed()
@@ -163,7 +169,7 @@
             arrive(run[part])
             total = spectra[part, pl.ds(my_tile, tile_units)]
             for o in range(n_tile - 1):
-                total = total + recv_tile[step, part, o]
+                total = total + recv_tile[step][part, o].astype(F32)
             half[part] = total
             source = half
             if half_send[step] is not None:
@@ -217,10 +223,10 @@
             for part in range(2):
                 arrive(run[part])
                 run[part] = gather(gathered.at[step, part], name, 2 * step + part)
+        low_stage("narrow")
         contraction = jnp.zeros_like(log_now)
         for part in range(2):
             arrive(run[part])
-            low_stage(("narrow", "tile")[part])
             for b, (g, c) in enumerate(blocks):
                 at = (slice(g * LANES, (g + 1) * LANES), slice(c * LANES, (c + 1) * LANES))
                 kernels[(part, *at)] = gathered[step, part, b * per_lane:(b + 1) * per_lane].reshape(LANES, LANES)
@@ -232,6 +238,7 @@
                 b = green_t[slice(ns + r, ns + r + wide_rows), :].astype(F32)
                 terms = a * from_a + b * from_b if part == 0 else b * from_a - a * from_b
                 contraction = contraction + jnp.sum(terms, axis=0, keepdims=True)
+        low_stage("tile")
         log_now = log_now - 0.5 * strength * contraction
         for copy in pending:
             copy.wait_send()
@@ -304,6 +311,7 @@
                 pltpu.VMEM((stations, points), BF16),
                 pltpu.VMEM((stations, points), BF16),
                 buf((2, all_units), F32),
+                tuple(None if k == F32 else buf((2, all_units), k) for k in send_types),
                 buf((2, tile_units), F32),
                 tuple(None if k == F32 else buf((2, tile_units), k) for k in send_types),
                 buf((2, narrow_units), F32),
@@ -314,7 +322,7 @@
                 buf((2, all_units), BF16),
                 pltpu.VMEM((slots, width, 2 * LANES), BF16),
                 pltpu.VMEM((slots, width, 2 * LANES), BF16),
-                buf((STEPS, 2, n_tile - 1, tile_units), F32),
+                tuple(buf((2, n_tile - 1, tile_units), k) for k in send_types),
                 tuple(buf((2, n_narrow - 1, narrow_units), k) for k in send_types),
                 tuple(buf((2, n_wide - 1, per), k) for k in send_types),
                 sems((2 * STEPS * per_pass,)),

time: 70.9 us -> 71.4 us (level)
  no operation moved by 1% of the time
where the time goes in v3:
time: 71.4 us; the launch traced here: 71.2 us
  Pallas kernels  67.6 us (95%)
  local copies, waits for them, and re-layouts  2.96 us (4%)
    pallas_call x1, Pallas kernels, on_device(): pl.pallas_call(functools.partial(kernel, sizes), out_shape=(jax.ShapeDtyp...  67.6 us
    unnamed x2, local copies, waits for them, and re-layouts  2.96 us

profile of v3, /device:TPU:0, one launch (start us, length us, event | category | flops | bytes accessed | tf_op | source)
XLA Modules:
  0.0 71.2 jit_solution(821427797665334357)
XLA Ops:
  0.6 67.6 %shard_map.77 = (f32[1,1024]{1,0:T(1,128)}, f32[132,512]{1,0:T(8,128)}) custom-call(bf16[1024,1024]{1,0:T(8,128)(2,1)} %green_ref.1, f32[1,1024]{1,0:T(1,128)} %bitcast.2, f32[528,512]{1,0:T(8,128)} %observed_ref.1, s32[528]{0:T(1024)} %owner_ref.1, s32[528]{0:T(1024)} %constant.4.clone.unit_ref, s32[528]{0:T(1024)} %constant.5.clone.lane_ref), custom_call_target="tpu_custom_call" | custom-call | tf_op jit(solution)/shard_map/pallas_call | solution.py:302
  68.3 1.3 %copy.10 = f32[1024]{0:T(1024)} copy(f32[1024]{0:T(1024)} %bitcast.3) | data formatting | bytes 8192
  69.6 1.7 %copy.11 = f32[132,512]{1,0:T(8,128)} copy(f32[132,512]{1,0:T(8,128)} %get-tuple-element.9) | data formatting | bytes 540672
